TPU v7x, 128 devices: a whole 4x4x4 slice. The times are simulated.
128 devices in a mesh: tile: 32 (over z_hi, x, y), blk: 4 (over z_lo, core).
Axes of the slice: x: 4, y: 4, z: 4 (z_hi: 2, z_lo: 2; z = z_hi * 2 + z_lo), core: 2. Of those that a mesh axis runs over, the one named last changes fastest.
Arguments:
- image_tokens: bfloat16 [16, 1024, 1536], P(None, 'tile', 'blk'), may hold values from -10 to 10
- text_tokens: bfloat16 [16, 160, 1536], P(None, 'tile', 'blk'), may hold values from -10 to 10
- step_index: int32 [16], replicated, may hold values from 0 to 27
- text_length: int32 [16], replicated, may hold values from 1 to 160, as said below
- image_table: bfloat16 [28, 6, 1536], replicated, may hold values from -3 to 3
- text_table: bfloat16 [28, 3, 1536], replicated, may hold values from -3 to 3
- qkv_image: bfloat16 [1536, 3, 1536], P(None, None, 'blk'), may hold values from -0.15625 to 0.15625
- qkv_text: bfloat16 [1536, 3, 1536], P(None, None, 'blk'), may hold values from -0.15625 to 0.15625
- attn_out_image: bfloat16 [1536, 1536], P('blk'), may hold values from -0.15625 to 0.15625
- attn_out_text: bfloat16 [1536, 1536], P('blk'), may hold values from -0.15625 to 0.15625
- query_gain_image: float32 [64], replicated, may hold values from 1 to 12
- key_gain_image: float32 [64], replicated, may hold values from 1 to 12
- query_gain_text: float32 [64], replicated, may hold values from 1 to 12
- key_gain_text: float32 [64], replicated, may hold values from 1 to 12
- up_weight: bfloat16 [1536, 6144], P(None, 'blk'), may hold values from -0.15625 to 0.15625
- down_weight: bfloat16 [6144, 1536], P('blk'), may hold values from -0.078125 to 0.078125
Outputs:
- image_out: bfloat16 [16, 1024, 1536], P(None, 'tile', 'blk')
- text_out: bfloat16 [16, 160, 1536], P(None, 'tile', 'blk')
Inputs may be any that keep to these rules, and one draw needn't show every extreme that they name: `text_length`: some request has all 160 slots valid.
All inputs are finite; a program needn't handle non-finite values.
Results may differ from a plain program's by a relative error of at most 0.015.
The roundings to bfloat16 on the way count: a program that leaves them out, or rounds other values in their place, can miss the bound.
Values may be sent and summed in bfloat16 or wider, within the bound.
No kernel may reach another device: no remote copies, remote signals or barrier semaphores. Data moves between devices by JAX's collectives and lax.ppermute only.
A program may use at most 192 MiB of HBM per device.

v0:
```python
import jax
import jax.numpy as jnp
from jax import lax
from jax.sharding import PartitionSpec as P

HEAD_DIM = 64
masked_score = -1e30


def layer_norm(values):
    centre = jnp.mean(values, axis=-1, keepdims=True)
    spread = jnp.mean(jnp.square(values - centre), axis=-1, keepdims=True)
    return (values - centre) * lax.rsqrt(spread + 1e-06)


def modulate(normed, shift_rows, scale_rows):
    return (normed * (1.0 + scale_rows[:, None, :]) + shift_rows[:, None, :]).astype(jnp.bfloat16)


def lookup(table_rows, step_index):
    picker = (step_index[:, None] == jnp.arange(table_rows.shape[0])[None, :]).astype(
        table_rows.dtype
    )
    return jnp.einsum("rs,skd->rkd", picker, table_rows, preferred_element_type=jnp.float32)


def head_norm(values, gain_vector):
    inverse_rms = lax.rsqrt(jnp.mean(jnp.square(values), axis=-1, keepdims=True) + 1e-06)
    return (values * inverse_rms * gain_vector).astype(jnp.bfloat16)


def project_heads(activations, weight, gain_query, gain_key):
    projected = jnp.einsum("rsd,dke->rske", activations, weight, preferred_element_type=jnp.float32)
    split_shape = projected.shape[:2] + (projected.shape[3] // HEAD_DIM, HEAD_DIM)
    query_heads = head_norm(projected[:, :, 0].reshape(split_shape), gain_query)
    key_heads = head_norm(projected[:, :, 1].reshape(split_shape), gain_key)
    value_heads = projected[:, :, 2].reshape(split_shape).astype(jnp.bfloat16)
    return (query_heads, key_heads, value_heads)


def per_device(
    image_tokens,
    text_tokens,
    step_index,
    text_length,
    image_table,
    text_table,
    qkv_image,
    qkv_text,
    attn_out_image,
    attn_out_text,
    query_gain_image,
    key_gain_image,
    query_gain_text,
    key_gain_text,
    up_weight,
    down_weight,
):
    requests = image_tokens.shape[0]
    image_rows = image_tokens.shape[1]
    text_rows = text_tokens.shape[1]
    joint_rows = image_rows + text_rows
    part_width = image_tokens.shape[2]
    column_start = lax.axis_index("blk") * part_width
    scale_factor = HEAD_DIM ** (-0.5)
    image_mods = lookup(image_table, step_index)
    text_mods = lookup(text_table, step_index)
    image_local = lax.dynamic_slice_in_dim(image_mods, column_start, part_width, 2)
    text_local = lax.dynamic_slice_in_dim(text_mods, column_start, part_width, 2)
    image_float = image_tokens.astype(jnp.float32)
    text_float = text_tokens.astype(jnp.float32)
    image_whole, text_whole = (
        lax.all_gather(image_tokens, "blk", axis=2, tiled=True),
        lax.all_gather(text_tokens, "blk", axis=2, tiled=True),
    )
    image_acts = modulate(
        layer_norm(image_whole.astype(jnp.float32)), image_mods[:, 0], image_mods[:, 1]
    )
    text_acts = modulate(
        layer_norm(text_whole.astype(jnp.float32)), text_mods[:, 0], text_mods[:, 1]
    )
    image_q, image_k, image_v = project_heads(
        image_acts, qkv_image, query_gain_image, key_gain_image
    )
    text_q, text_k, text_v = project_heads(text_acts, qkv_text, query_gain_text, key_gain_text)
    joint_q = jnp.concatenate([image_q, text_q], axis=1)
    joint_k = jnp.concatenate([image_k, text_k], axis=1)
    joint_v = jnp.concatenate([image_v, text_v], axis=1)
    head_count = joint_q.shape[2]
    key_value = jnp.stack(
        [
            joint_k.reshape(requests, joint_rows, part_width),
            joint_v.reshape(requests, joint_rows, part_width),
        ],
        axis=2,
    )
    shard_piece = lax.all_gather(key_value, "tile", axis=1, tiled=True)
    running_max = jnp.full((requests, head_count, joint_rows, 1), masked_score, jnp.float32)
    piece_rows = shard_piece.shape[1]
    position = jnp.arange(piece_rows, dtype=jnp.int32)
    offset = position % joint_rows
    text_slot = position // joint_rows * text_rows + offset - image_rows
    visible = (offset < image_rows)[None, :] | (text_slot[None, :] < text_length[:, None])
    piece_keys = shard_piece[:, :, 0].reshape(requests, piece_rows, head_count, HEAD_DIM)
    piece_values = shard_piece[:, :, 1].reshape(requests, piece_rows, head_count, HEAD_DIM)
    scores = (
        jnp.einsum("rqhe,rkhe->rhqk", joint_q, piece_keys, preferred_element_type=jnp.float32)
        * scale_factor
    )
    visible_mask = visible[:, None, None, :]
    new_max = jnp.maximum(
        running_max, jnp.max(jnp.where(visible_mask, scores, masked_score), axis=-1, keepdims=True)
    )
    weights = jnp.where(visible_mask, jnp.exp(scores - new_max), 0.0)
    running_sum = jnp.sum(weights, axis=-1, keepdims=True)
    running_out = jnp.einsum(
        "rhqk,rkhe->rhqe",
        weights.astype(jnp.bfloat16),
        piece_values,
        preferred_element_type=jnp.float32,
    )
    attended = (
        jnp.transpose(running_out / running_sum, (0, 2, 1, 3))
        .astype(jnp.bfloat16)
        .reshape(requests, joint_rows, part_width)
    )
    image_term = jnp.einsum(
        "rsd,de->rse", attended[:, :image_rows], attn_out_image, preferred_element_type=jnp.float32
    )
    text_term = jnp.einsum(
        "rsd,de->rse", attended[:, image_rows:], attn_out_text, preferred_element_type=jnp.float32
    )
    image_proj, text_proj = (
        lax.psum_scatter(
            image_term.astype(jnp.bfloat16), "blk", scatter_dimension=2, tiled=True
        ).astype(jnp.float32),
        lax.psum_scatter(
            text_term.astype(jnp.bfloat16), "blk", scatter_dimension=2, tiled=True
        ).astype(jnp.float32),
    )
    image_mid = (image_float + image_local[:, 2][:, None, :] * image_proj).astype(jnp.bfloat16)
    text_out = (text_float + text_local[:, 2][:, None, :] * text_proj).astype(jnp.bfloat16)
    middle_float = image_mid.astype(jnp.float32)
    middle_whole = lax.all_gather(image_mid, "blk", axis=2, tiled=True)
    mlp_input = modulate(
        layer_norm(middle_whole.astype(jnp.float32)), image_mods[:, 3], image_mods[:, 4]
    )
    hidden = jax.nn.gelu(
        jnp.einsum("rsd,df->rsf", mlp_input, up_weight, preferred_element_type=jnp.float32),
        approximate=True,
    ).astype(jnp.bfloat16)
    down_term = jnp.einsum("rsf,fd->rsd", hidden, down_weight, preferred_element_type=jnp.float32)
    down_sum = lax.psum_scatter(
        down_term.astype(jnp.bfloat16), "blk", scatter_dimension=2, tiled=True
    ).astype(jnp.float32)
    image_out = (middle_float + image_local[:, 5][:, None, :] * down_sum).astype(jnp.bfloat16)
    return (image_out, text_out)


def solution(mesh):
    in_specs = (
        P(None, "tile", "blk"),
        P(None, "tile", "blk"),
        P(),
        P(),
        P(),
        P(),
        P(None, None, "blk"),
        P(None, None, "blk"),
        P("blk", None),
        P("blk", None),
        P(),
        P(),
        P(),
        P(),
        P(None, "blk"),
        P("blk", None),
    )
    out_specs = (P(None, "tile", "blk"), P(None, "tile", "blk"))
    return jax.shard_map(
        per_device, mesh=mesh, in_specs=in_specs, out_specs=out_specs, check_vma=False
    )
```

profile of v0, /device:TPU:1, one launch (start us, length us, event | category | flops | bytes accessed | tf_op | source)
XLA Modules:
  0.0 523.8 jit_solution(4415324707470170074)
XLA Ops:
  9.7 7.6 %all_gather.13 = bf16[16,5,1536]{2,0,1:T(8,128)(2,1)S(1)} all-gather(bf16[16,5,384]{2,0,1:T(8,128)(2,1)} %param.17), channel_id=1, replica_groups=mesh['tile'=32,'blk'=4] {'blk'}, dimensions={2}, use_global_device_ids=true | all-gather | bytes 307200 | tf_op jit(solution)/shard_map/all_gather | solution.py:74
  19.6 2.8 fusion.16
  42.1 2.4 fusion.18
  55.6 230.7 %all-gather.6.cloned.1.call-done = bf16[16,1184,2,384]{3,0,2,1:T(8,128)(2,1)} async-done(((bf16[16,37,2,384]{3,0,2,1:T(8,128)(2,1)}), bf16[16,1184,2,384]{3,0,2,1:T(8,128)(2,1)}) %all-gather.6.cloned.1.call-update) | async-done | bytes 29098000 | tf_op jit(solution)/shard_map/all_gather | solution.py:97
  286.4 21.9 %fusion.114 = (bf16[16,1184,1,384]{3,0,2,1:T(8,128)(2,1)}, bf16[16,1184,1,384]{3,0,2,1:T(8,128)(2,1)}) fusion(bf16[16,1184,2,384]{3,0,2,1:T(8,128)(2,1)} %all-gather.6.cloned.1.call-done), kind=kLoop, calls=%fused_computation.149 | loop fusion | bytes 58195968 | tf_op jit(solution)/shard_map/slice | solution.py:104
  308.2 20.2 %copy.78 = bf16[16,1184,1,384]{1,3,0,2:T(8,128)(2,1)} copy(bf16[16,1184,1,384]{3,0,2,1:T(8,128)(2,1)} %get-tuple-element.2) | data formatting | bytes 29097984
  328.5 12.2 %select_reduce_fusion = (f32[16,6,37]{2,1,0:T(8,128)S(1)}, f32[16,6,37,1184]{3,2,1,0:T(8,128)}) fusion(pred[16,1184]{1,0:T(8,128)(4,1)S(1)} %compare_or_fusion, bf16[16,1184,6,64]{1,3,2,0:T(8,128)(2,1)} %bitcast.109, bf16[16,5,6,64]{3,1,2,0:T(8,128)(2,1)S(1)} %fusion.79, bf16[16,32,6,64]{3,1,2,0:T(8,128)(2,1)S(1)} %fusion.50), kind=kOutput, calls=%fused_computation.1 | convolution fusion | flops 551835136 | bytes 31859072 | tf_op jit(solution)/shard_map/rqhe,rkhe->rhqk/dot_general | solution.py:107
  340.7 20.2 %copy.79 = bf16[16,1184,1,384]{1,3,0,2:T(8,128)(2,1)} copy(bf16[16,1184,1,384]{3,0,2,1:T(8,128)(2,1)} %get-tuple-element.3) | data formatting | bytes 29097984
  360.9 9.8 %fusion = f32[16,6,37]{2,1,0:T(8,128)S(1)} fusion(f32[16,6,37,1184]{3,2,1,0:T(8,128)} %get-tuple-element.17, f32[16,6,37]{2,1,0:T(8,128)S(1)} %broadcast_maximum_fusion, pred[16,1184]{1,0:T(8,128)(4,1)S(1)} %compare_or_fusion), kind=kLoop, calls=%fused_computation.2 | loop fusion | flops 16818720 | bytes 16869632 | tf_op jit(solution)/shard_map/reduce_sum | solution.py:115
  370.7 13.1 %fusion.43 = bf16[16,37,6,64]{3,1,2,0:T(8,128)(2,1)S(1)} fusion(bf16[16,1184,6,64]{1,3,2,0:T(8,128)(2,1)} %bitcast.112, f32[16,6,37,1184]{3,2,1,0:T(8,128)} %get-tuple-element.17, f32[16,6,37]{2,1,0:T(8,128)S(1)} %broadcast_maximum_fusion, pred[16,1184]{1,0:T(8,128)(4,1)S(1)} %compare_or_fusion, f32[16,37,6]{1,2,0:T(8,128)S(1)} %bitcast.117), kind=kOutput, calls=%fused_computation.47 | convolution fusion | flops 555589632 | bytes 31873280 | tf_op jit(solution)/shard_map/rhqk,rkhe->rhqe/dot_general | solution.py:116
  385.0 2.3 convolution_convert_fusion
  387.2 6.6 %copy.72 = bf16[16,32,1536]{1,0,2:T(8,128)(2,1)} copy(bf16[16,32,1536]{2,1,0:T(8,128)(2,1)S(1)} %convolution_convert_fusion) | data formatting | bytes 3145728
  393.8 9.3 %reshape.168 = bf16[1536,512]{1,0:T(8,128)(2,1)} reshape(bf16[1536,16,32]{2,1,0:T(8,128)(2,1)} %bitcast.110) | data formatting | bytes 3145728
  404.8 20.8 %reduce-scatter.10.cloned.1.call-done = bf16[384,512]{1,0:T(8,128)(2,1)} async-done(((bf16[1536,512]{1,0:T(8,128)(2,1)}), bf16[384,512]{1,0:T(8,128)(2,1)}) %reduce-scatter.10.cloned.1.call-update) | async-done | bytes 393232
  431.4 2.4 copy.76
  433.8 2.4 reshape.172
  436.2 19.6 %all-gather.8.cloned.1.call-done = bf16[16,32,1536]{2,1,0:T(8,128)(2,1)} async-done(((bf16[16,32,384]{2,1,0:T(8,128)(2,1)}), bf16[16,32,1536]{2,1,0:T(8,128)(2,1)}) %all-gather.8.cloned.1.call-update) | async-done | bytes 1572880 | tf_op jit(solution)/shard_map/all_gather | solution.py:144
  459.7 8.9 %fusion.37 = bf16[16,32,1536]{2,1,0:T(8,128)(2,1)S(1)} fusion(bf16[1536,1536]{1,0:T(8,128)(2,1)} %param.31, bf16[1536,1536]{1,0:T(8,128)(2,1)} %param.30, bf16[16,32,1536]{2,1,0:T(8,128)(2,1)S(1)} %copy-done.3, f32[16,1536]{1,0:T(8,128)S(1)} %copy-done.14, f32[16,1536]{1,0:T(8,128)S(1)} %copy-done.13, f32[16,32]{1,0:T(8,128)S(1)} %add_rsqrt_fusion.4, ...), kind=kOutput, calls=%fused_computation.41 | convolution fusion | flops 4844421120 | bytes 12783616 | tf_op jit(solution)/shard_map/rsf,fd->rsd/dot_general | solution.py:152
  468.6 6.6 %copy.74 = bf16[16,32,1536]{1,0,2:T(8,128)(2,1)} copy(bf16[16,32,1536]{2,1,0:T(8,128)(2,1)S(1)} %fusion.37) | data formatting | bytes 3145728
  475.2 9.3 %reshape.170 = bf16[1536,512]{1,0:T(8,128)(2,1)} reshape(bf16[1536,16,32]{2,1,0:T(8,128)(2,1)} %bitcast.111) | data formatting | bytes 3145728
  484.6 2.3 reshape.173
  490.4 19.0 %reduce-scatter.12.cloned.1.call-done = bf16[384,512]{1,0:T(8,128)(2,1)} async-done(((bf16[1536,512]{1,0:T(8,128)(2,1)}), bf16[384,512]{1,0:T(8,128)(2,1)}) %reduce-scatter.12.cloned.1.call-update) | async-done | bytes 393232
  509.5 2.9 reshape.171
  512.3 2.6 copy.75
  (124 shorter events, 53.1 us)
Async XLA Ops:
  7.2 34.9 %copy-start = (bf16[1536,3,384]{2,0,1:T(8,128)(2,1)S(1)}, bf16[1536,3,384]{2,0,1:T(8,128)(2,1)}, u32[]{:S(2)}) copy-start(bf16[1536,3,384]{2,0,1:T(8,128)(2,1)} %param.22) | copy-start | bytes 10616836
  7.2 31.0 %all-gather.4.cloned.1.call-start = ((), (), s32[]{:S(2)}) async-start(), calls=%async_computation.3 | async-start | bytes 1966080 | tf_op jit(solution)/shard_map/all_gather | solution.py:73
  7.9 278.4 %all-gather.6.cloned.1.call-start = ((), (), s32[]{:S(2)}) async-start(), calls=%async_computation.4 | async-start | bytes 30007296 | tf_op jit(solution)/shard_map/all_gather | solution.py:97
  19.6 13.5 %copy-start.17 = (s32[16]{0:T(128)S(1)}, s32[16]{0:T(128)}, u32[]{:S(2)}) copy-start(s32[16]{0:T(128)} %param.18) | copy-start | bytes 196
  38.2 3.8 copy-start.2
  38.2 3.8 copy-start.15
  38.2 3.8 copy-start.16
  44.5 1.5 copy-start.4
  48.2 3.2 copy-start.11
  49.5 1.9 copy-start.7
  49.6 1.9 copy-start.12
  51.4 1.6 copy-start.10
  51.4 2.1 copy-start.20
  51.4 2.3 copy-start.18
  52.7 372.9 %reduce-scatter.10.cloned.1.call-start = ((), (), s32[]{:S(2)}) async-start(), calls=%async_computation.6 | async-start | bytes 1966080
  53.5 1.6 copy-start.19
  403.1 25.7 %copy-start.6 = (bf16[16,32,384]{2,1,0:T(8,128)(2,1)S(1)}, bf16[16,32,384]{2,1,0:T(8,128)(2,1)}, u32[]{:S(2)}) copy-start(bf16[16,32,384]{2,1,0:T(8,128)(2,1)} %param.16) | copy-start | bytes 1179652
  403.2 52.7 %all-gather.8.cloned.1.call-start = ((), (), s32[]{:S(2)}) async-start(), calls=%async_computation.5 | async-start | bytes 1966080 | tf_op jit(solution)/shard_map/all_gather | solution.py:144
  429.7 54.8 %reduce-scatter.14.cloned.1.call-start = ((), (), s32[]{:S(2)}) async-start(), calls=%async_computation.8 | async-start | bytes 491520
  433.8 25.9 %copy-start.13 = (f32[16,1536]{1,0:T(8,128)S(1)}, f32[16,1536]{1,0:T(8,128)}, u32[]{:S(2)}) copy-start(f32[16,1536]{1,0:T(8,128)} %get-tuple-element.8) | copy-start | bytes 294916
  433.8 25.9 %copy-start.14 = (f32[16,1536]{1,0:T(8,128)S(1)}, f32[16,1536]{1,0:T(8,128)}, u32[]{:S(2)}) copy-start(f32[16,1536]{1,0:T(8,128)} %get-tuple-element.9) | copy-start | bytes 294916
  436.2 73.3 %reduce-scatter.12.cloned.1.call-start = ((), (), s32[]{:S(2)}) async-start(), calls=%async_computation.7 | async-start | bytes 1966080
  455.9 3.8 copy-start.3
  484.5 32.4 %copy-start.1 = (bf16[1536,3,384]{2,0,1:T(8,128)(2,1)S(1)}, bf16[1536,3,384]{2,0,1:T(8,128)(2,1)}, u32[]{:S(2)}) copy-start(bf16[1536,3,384]{2,0,1:T(8,128)(2,1)} %param.22) | copy-start | bytes 10616836
  (3 other events, 2.3 us)
Sparse Core Ops, SparseCore 0:
  9.7 28.4 all-gather.3
  52.9 233.4 all-gather.5
  403.3 22.3 reduce-scatter.9
  429.8 25.9 all-gather.7
  458.1 18.7 reduce-scatter.13
  484.6 24.7 reduce-scatter.11
where the time goes:
time: 526 us; the launch traced here: 524 us
  waiting for transfers between devices  293 us (56%)
  local copies, waits for them, and re-layouts  130 us (25%)
  matrix products  45.9 us (9%)
  other arithmetic  32 us (6%)
  between operations  14.6 us (3%)
  blocking collectives  7.62 us (1%)
    all_gather x1, waiting for transfers between devices, per_device(): shard_piece = lax.all_gather(key_value, 'tile', axis=1, tiled=True)  231 us
    unnamed x56, local copies, waits for them, and re-layouts  92.3 us
    unnamed x9, waiting for transfers between devices  40.6 us
    slice x1, local copies, waits for them, and re-layouts, per_device(): shard_piece[:, :, 0].reshape(requests, piece_rows, head_count, HEAD_DIM)  21.9 us
    all_gather x1, waiting for transfers between devices, per_device(): middle_whole = lax.all_gather(image_mid, 'blk', axis=2, tiled=True)  19.6 us
    dot_general x1, matrix products, per_device(): jnp.einsum('rhqk,rkhe->rhqe', weights.astype(jnp.bfloat16), piece_values,...  13.1 us
    dot_general x1, matrix products, per_device(): jnp.einsum('rqhe,rkhe->rhqk', joint_q, piece_keys, preferred_element_type...  12.2 us
  transfers between devices with their start and end apart: 6, of which 5 were waited for; matrix products, arithmetic and copies ran while one was open for 12% of the time, Pallas kernels for 0%

commit v1 on v0

--- a/solution.py
+++ b/solution.py
@@ -2,9 +2,16 @@
 import jax.numpy as jnp
 from jax import lax
 from jax.sharding import PartitionSpec as P
+from jax.lax import all_to_all, axis_size
 
 HEAD_DIM = 64
 masked_score = -1e30
+
+
+def reach_seats_all_in(obj, peer_axis):
+    s_next = jnp.stack(axis_size(peer_axis) * [obj])
+    state_now = all_to_all(s_next, peer_axis, split_axis=0, concat_axis=0)
+    return jnp.concatenate(state_now, 1)
 
 
 def layer_norm(values):
@@ -94,7 +101,7 @@
         ],
         axis=2,
     )
-    shard_piece = lax.all_gather(key_value, "tile", axis=1, tiled=True)
+    shard_piece = reach_seats_all_in(key_value, peer_axis="tile")
     running_max = jnp.full((requests, head_count, joint_rows, 1), masked_score, jnp.float32)
     piece_rows = shard_piece.shape[1]
     position = jnp.arange(piece_rows, dtype=jnp.int32)

time: 526 us -> 866 us (1.65)
  waiting for transfers between devices: 293 us -> 615 us
  starting transfers between devices: 0.64 us -> 9.98 us
  local copies, waits for them, and re-layouts: 130 us -> 139 us
    all_to_all x0 -> x1, waiting for transfers between devices: none -> 463 us  [reach_seats_all_in(): state_now = all_to_all(s_next, peer_axis, split_axis=0, concat_axis=0)]
    all_gather x1 -> x0, waiting for transfers between devices: 231 us -> none  [per_device(): shard_piece = lax.all_gather(key_value, 'tile', axis=1, tiled=True)]
    unnamed x9 -> x8, waiting for transfers between devices: 40.6 us -> 131 us
    unnamed x56 -> x54, local copies, waits for them, and re-layouts: 92.3 us -> 51.9 us
    slice x1 -> x2, local copies, waits for them, and re-layouts: 21.9 us -> 42.1 us  [per_device(): shard_piece[:, :, 0].reshape(requests, piece_rows, head_count, HEAD_DIM)]
    slice x0 -> x1, local copies, waits for them, and re-layouts: none -> 20.2 us  [per_device(): shard_piece[:, :, 1].reshape(requests, piece_rows, head_count, HEAD_DIM)]
    another operation x0 -> x1, local copies, waits for them, and re-layouts: none -> 9.8 us  [reach_seats_all_in(): s_next = jnp.stack(axis_size(peer_axis) * [obj])]
    all_to_all x0 -> x1, starting transfers between devices: none -> 9.37 us  [reach_seats_all_in(): state_now = all_to_all(s_next, peer_axis, split_axis=0, concat_axis=0)]
  transfers between devices with their start and end apart: 6 -> 6, of which waited for: 5 -> 5; matrix products, arithmetic and copies ran while one was open for 12% -> 7% of each run, Pallas kernels for 0% -> 0%
where the time goes in v1:
time: 866 us; the launch traced here: 864 us
  waiting for transfers between devices  615 us (71%)
  local copies, waits for them, and re-layouts  139 us (16%)
  matrix products  45.8 us (5%)
  other arithmetic  32 us (4%)
  between operations  14.3 us (2%)
  starting transfers between devices  9.98 us (1%)
    all_to_all x1, waiting for transfers between devices, reach_seats_all_in(): state_now = all_to_all(s_next, peer_axis, split_axis=0, concat_axis=0)  463 us
    unnamed x8, waiting for transfers between devices  131 us
    unnamed x54, local copies, waits for them, and re-layouts  51.9 us
    slice x2, local copies, waits for them, and re-layouts, per_device(): shard_piece[:, :, 0].reshape(requests, piece_rows, head_count, HEAD_DIM)  42.1 us
    slice x1, local copies, waits for them, and re-layouts, per_device(): shard_piece[:, :, 1].reshape(requests, piece_rows, head_count, HEAD_DIM)  20.2 us
    all_gather x1, waiting for transfers between devices, per_device(): middle_whole = lax.all_gather(image_mid, 'blk', axis=2, tiled=True)  19.6 us
  transfers between devices with their start and end apart: 6, of which 5 were waited for; matrix products, arithmetic and copies ran while one was open for 7% of the time, Pallas kernels for 0%

profile of v1, /device:TPU:1, one launch (start us, length us, event | category | flops | bytes accessed | tf_op | source)
XLA Modules:
  0.0 863.9 jit_solution(13629913809127929448)
XLA Ops:
  9.7 7.6 all_gather.10
  19.7 2.8 fusion.16
  42.1 2.4 fusion.18
  51.7 9.8 %stack.5 = bf16[32,16,37,2,384]{4,1,3,2,0:T(8,128)(2,1)} broadcast(bf16[16,37,2,384]{3,0,2,1:T(8,128)(2,1)S(1)} %copy.65), dimensions={1,2,3,4} | broadcast | bytes 30007296 | tf_op jit(solution)/shard_map/stack | solution.py:12
  61.5 9.4 %all-to-all-start = ((bf16[32,16,37,2,384]{4,1,3,2,0:T(8,128)(2,1)}), bf16[32,16,37,2,384]{4,1,3,2,0:T(8,128)(2,1)}, u32[]{:S(2)}, u32[]{:S(2)}) async-start(bf16[32,16,37,2,384]{4,1,3,2,0:T(8,128)(2,1)} %stack.5), calls=%async_computation | async-start | bytes 58195968 | tf_op jit(solution)/shard_map/all_to_all | solution.py:13
  73.8 463.1 %all-to-all-done = bf16[32,16,37,2,384]{4,1,3,2,0:T(8,128)(2,1)} async-done(((bf16[32,16,37,2,384]{4,1,3,2,0:T(8,128)(2,1)}), bf16[32,16,37,2,384]{4,1,3,2,0:T(8,128)(2,1)}, u32[]{:S(2)}, u32[]{:S(2)}) %all-to-all-start) | async-done | bytes 29098016 | tf_op jit(solution)/shard_map/all_to_all | solution.py:13
  536.9 21.9 %fusion.114 = (bf16[16,1184,1,384]{3,0,2,1:T(8,128)(2,1)}, bf16[16,1184,1,384]{3,0,2,1:T(8,128)(2,1)}) fusion(bf16[16,1184,2,384]{3,0,2,1:T(8,128)(2,1)} %bitcast.15), kind=kLoop, calls=%fused_computation.149 | loop fusion | bytes 58195968 | tf_op jit(solution)/shard_map/slice | solution.py:111
  558.8 20.2 %copy.66 = bf16[16,1184,1,384]{1,3,0,2:T(8,128)(2,1)} copy(bf16[16,1184,1,384]{3,0,2,1:T(8,128)(2,1)} %get-tuple-element.2) | data formatting | bytes 29097984 | tf_op jit(solution)/shard_map/slice | solution.py:111
  579.0 12.2 %select_reduce_fusion = (f32[16,6,37]{2,1,0:T(8,128)S(1)}, f32[16,6,37,1184]{3,2,1,0:T(8,128)}) fusion(pred[16,1184]{1,0:T(8,128)(4,1)S(1)} %compare_or_fusion, bf16[16,1184,6,64]{1,3,2,0:T(8,128)(2,1)} %bitcast.112, bf16[16,5,6,64]{3,1,2,0:T(8,128)(2,1)S(1)} %fusion.79, bf16[16,32,6,64]{3,1,2,0:T(8,128)(2,1)S(1)} %fusion.50), kind=kOutput, calls=%fused_computation.1 | convolution fusion | flops 551835136 | bytes 31859072 | tf_op jit(solution)/shard_map/rqhe,rkhe->rhqk/dot_general | solution.py:114
  591.2 20.2 %copy.67 = bf16[16,1184,1,384]{1,3,0,2:T(8,128)(2,1)} copy(bf16[16,1184,1,384]{3,0,2,1:T(8,128)(2,1)} %get-tuple-element.3) | data formatting | bytes 29097984 | tf_op jit(solution)/shard_map/slice | solution.py:112
  611.4 9.8 %fusion = f32[16,6,37]{2,1,0:T(8,128)S(1)} fusion(f32[16,6,37,1184]{3,2,1,0:T(8,128)} %get-tuple-element.17, f32[16,6,37]{2,1,0:T(8,128)S(1)} %broadcast_maximum_fusion, pred[16,1184]{1,0:T(8,128)(4,1)S(1)} %compare_or_fusion), kind=kLoop, calls=%fused_computation.2 | loop fusion | flops 16818720 | bytes 16869632 | tf_op jit(solution)/shard_map/reduce_sum | solution.py:122
  621.2 13.1 %fusion.43 = bf16[16,37,6,64]{3,1,2,0:T(8,128)(2,1)S(1)} fusion(bf16[16,1184,6,64]{1,3,2,0:T(8,128)(2,1)} %bitcast.115, f32[16,6,37,1184]{3,2,1,0:T(8,128)} %get-tuple-element.17, f32[16,6,37]{2,1,0:T(8,128)S(1)} %broadcast_maximum_fusion, pred[16,1184]{1,0:T(8,128)(4,1)S(1)} %compare_or_fusion, f32[16,37,6]{1,2,0:T(8,128)S(1)} %bitcast.120), kind=kOutput, calls=%fused_computation.47 | convolution fusion | flops 555589632 | bytes 31873280 | tf_op jit(solution)/shard_map/rhqk,rkhe->rhqe/dot_general | solution.py:123
  637.7 6.6 copy.72
  644.3 9.3 %reshape.178 = bf16[1536,512]{1,0:T(8,128)(2,1)} reshape(bf16[1536,16,32]{2,1,0:T(8,128)(2,1)} %bitcast.113) | data formatting | bytes 3145728
  655.3 110.8 %reduce-scatter.10.cloned.1.call-done = bf16[384,512]{1,0:T(8,128)(2,1)} async-done(((bf16[1536,512]{1,0:T(8,128)(2,1)}), bf16[384,512]{1,0:T(8,128)(2,1)}) %reduce-scatter.10.cloned.1.call-update) | async-done | bytes 393232
  771.8 2.4 copy.76
  774.2 2.4 reshape.182
  776.7 19.6 %all-gather.5.cloned.1.call-done = bf16[16,32,1536]{2,1,0:T(8,128)(2,1)} async-done(((bf16[16,32,384]{2,1,0:T(8,128)(2,1)}), bf16[16,32,1536]{2,1,0:T(8,128)(2,1)}) %all-gather.5.cloned.1.call-update) | async-done | bytes 1572880 | tf_op jit(solution)/shard_map/all_gather | solution.py:151
  800.1 8.9 %fusion.37 = bf16[16,32,1536]{2,1,0:T(8,128)(2,1)S(1)} fusion(bf16[1536,1536]{1,0:T(8,128)(2,1)} %param.31, bf16[1536,1536]{1,0:T(8,128)(2,1)} %param.30, bf16[16,32,1536]{2,1,0:T(8,128)(2,1)S(1)} %copy-done.3, f32[16,1536]{1,0:T(8,128)S(1)} %copy-done.14, f32[16,1536]{1,0:T(8,128)S(1)} %copy-done.13, f32[16,32]{1,0:T(8,128)S(1)} %add_rsqrt_fusion.4, ...), kind=kOutput, calls=%fused_computation.41 | convolution fusion | flops 4844421120 | bytes 12783616 | tf_op jit(solution)/shard_map/rsf,fd->rsd/dot_general | solution.py:159
  809.0 6.6 copy.74
  815.6 9.3 %reshape.180 = bf16[1536,512]{1,0:T(8,128)(2,1)} reshape(bf16[1536,16,32]{2,1,0:T(8,128)(2,1)} %bitcast.114) | data formatting | bytes 3145728
  830.8 19.0 %reduce-scatter.12.cloned.1.call-done = bf16[384,512]{1,0:T(8,128)(2,1)} async-done(((bf16[1536,512]{1,0:T(8,128)(2,1)}), bf16[384,512]{1,0:T(8,128)(2,1)}) %reduce-scatter.12.cloned.1.call-update) | async-done | bytes 393232
  849.8 2.9 reshape.181
  852.7 2.6 copy.75
  (124 shorter events, 56.7 us)
Async XLA Ops:
  7.2 34.9 %copy-start = (bf16[1536,3,384]{2,0,1:T(8,128)(2,1)S(1)}, bf16[1536,3,384]{2,0,1:T(8,128)(2,1)}, u32[]{:S(2)}) copy-start(bf16[1536,3,384]{2,0,1:T(8,128)(2,1)} %param.22) | copy-start | bytes 10616836
  7.2 31.0 %all-gather.3.cloned.1.call-start = ((), (), s32[]{:S(2)}) async-start(), calls=%async_computation.4 | async-start | bytes 1966080 | tf_op jit(solution)/shard_map/all_gather | solution.py:80
  19.6 13.5 %copy-start.17 = (s32[16]{0:T(128)S(1)}, s32[16]{0:T(128)}, u32[]{:S(2)}) copy-start(s32[16]{0:T(128)} %param.18) | copy-start | bytes 196
  38.2 3.8 copy-start.2
  38.2 3.8 copy-start.15
  38.2 3.8 copy-start.16
  44.5 1.5 copy-start.4
  48.1 3.2 copy-start.11
  48.2 3.2 copy-start.12
  49.6 1.8 copy-start.7
  61.5 9.6 %copy-start.10 = (f32[16,5,1,384]{3,0,2,1:T(8,128)S(1)}, f32[16,5,1,384]{3,0,2,1:T(8,128)}, u32[]{:S(2)}) copy-start(f32[16,5,1,384]{3,0,2,1:T(8,128)} %get-tuple-element.12) | copy-start | bytes 368644
  61.5 10.2 %copy-start.20 = (f32[64]{0:T(128)S(1)}, f32[64]{0:T(128)}, u32[]{:S(2)}) copy-start(f32[64]{0:T(128)} %param.28) | copy-start | bytes 772
  61.5 10.4 %copy-start.18 = (s32[16]{0:T(128)S(1)}, s32[16]{0:T(128)}, u32[]{:S(2)}) copy-start(s32[16]{0:T(128)} %param.19) | copy-start | bytes 196
  61.5 475.4 %all-to-all-start = ((bf16[32,16,37,2,384]{4,1,3,2,0:T(8,128)(2,1)}), bf16[32,16,37,2,384]{4,1,3,2,0:T(8,128)(2,1)}, u32[]{:S(2)}, u32[]{:S(2)}) async-start(bf16[32,16,37,2,384]{4,1,3,2,0:T(8,128)(2,1)} %stack.5), calls=%async_computation | async-start | bytes 58195968 | tf_op jit(solution)/shard_map/all_to_all | solution.py:13
  70.9 695.2 %reduce-scatter.10.cloned.1.call-start = ((), (), s32[]{:S(2)}) async-start(), calls=%async_computation.6 | async-start | bytes 1966080
  71.7 1.6 copy-start.19
  653.6 115.7 %copy-start.6 = (bf16[16,32,384]{2,1,0:T(8,128)(2,1)S(1)}, bf16[16,32,384]{2,1,0:T(8,128)(2,1)}, u32[]{:S(2)}) copy-start(bf16[16,32,384]{2,1,0:T(8,128)(2,1)} %param.16) | copy-start | bytes 1179652
  653.6 142.7 %all-gather.5.cloned.1.call-start = ((), (), s32[]{:S(2)}) async-start(), calls=%async_computation.5 | async-start | bytes 1966080 | tf_op jit(solution)/shard_map/all_gather | solution.py:151
  770.2 54.8 %reduce-scatter.14.cloned.1.call-start = ((), (), s32[]{:S(2)}) async-start(), calls=%async_computation.8 | async-start | bytes 491520
  774.2 25.8 %copy-start.13 = (f32[16,1536]{1,0:T(8,128)S(1)}, f32[16,1536]{1,0:T(8,128)}, u32[]{:S(2)}) copy-start(f32[16,1536]{1,0:T(8,128)} %get-tuple-element.8) | copy-start | bytes 294916
  774.2 25.8 %copy-start.14 = (f32[16,1536]{1,0:T(8,128)S(1)}, f32[16,1536]{1,0:T(8,128)}, u32[]{:S(2)}) copy-start(f32[16,1536]{1,0:T(8,128)} %get-tuple-element.9) | copy-start | bytes 294916
  776.6 73.2 %reduce-scatter.12.cloned.1.call-start = ((), (), s32[]{:S(2)}) async-start(), calls=%async_computation.7 | async-start | bytes 1966080
  796.3 3.8 copy-start.3
  825.0 32.4 %copy-start.1 = (bf16[1536,3,384]{2,0,1:T(8,128)(2,1)S(1)}, bf16[1536,3,384]{2,0,1:T(8,128)(2,1)}, u32[]{:S(2)}) copy-start(bf16[1536,3,384]{2,0,1:T(8,128)(2,1)} %param.22) | copy-start | bytes 10616836
  (3 other events, 2.4 us)
Sparse Core Ops, SparseCore 0:
  9.7 28.4 all-gather.2
  653.7 112.3 reduce-scatter.9
  770.3 25.9 all-gather.4
  798.5 18.7 reduce-scatter.13
  825.1 24.7 reduce-scatter.11
